TPU v7x, 768 devices: a whole 4x8x12 slice. The times are simulated.
768 devices in a mesh: island: 16 (over x_hi, y), fsdp: 12 (over z), tensor: 4 (over x_lo, core).
Axes of the slice: x: 4 (x_hi: 2, x_lo: 2; x = x_hi * 2 + x_lo), y: 8, z: 12, core: 2. Of those that a mesh axis runs over, the one named last changes fastest.
Arguments:
- tokens: bfloat16 [24576, 6144], P(('island', 'fsdp')), may hold values from -6 to 6
- key_weight: bfloat16 [16, 6144, 1024], P('island', 'fsdp', 'tensor'), may hold values from -0.078125 to 0.078125
- key_cotangent: bfloat16 [24576, 1024], P(('island', 'fsdp'), 'tensor'), may hold values from -6 to 6
- local_frag: bfloat16 [16, 2, 6144, 2048], P('island', None, 'fsdp', 'tensor'), may hold values from -6 to 6
- outer_frag: float32 [2, 6144, 2048], P(None, 'fsdp', 'tensor'), may hold values from -6 to 6
- momentum: float32 [2, 6144, 2048], P(None, 'fsdp', 'tensor'), may hold values from -6 to 6
Outputs:
- keys: bfloat16 [24576, 1024], P(('island', 'fsdp'), 'tensor')
- input_grad: bfloat16 [24576, 6144], P(('island', 'fsdp', 'tensor'))
- weight_grad: bfloat16 [16, 6144, 1024], P('island', 'fsdp', 'tensor')
- new_outer: float32 [2, 6144, 2048], P(None, 'fsdp', 'tensor')
- new_momentum: float32 [2, 6144, 2048], P(None, 'fsdp', 'tensor')
All inputs are finite; a program needn't handle non-finite values.
Results may differ from a plain program's by a relative error of at most 0.015.
Values may be sent and summed in bfloat16 or wider, within the bound.
A program may use at most 64 MiB of HBM per device.

v0:
```python
import jax
import jax.numpy as jnp
from jax import lax
from jax.sharding import PartitionSpec as P

outer_rate = 0.7
beta_outer = 0.9


def body(tokens, key_weight, key_cotangent, local_frag, outer_frag, momentum):
    own_shard = key_weight[0]
    gathered = lax.all_gather(own_shard, "fsdp", axis=0, tiled=True)
    keys = jnp.dot(tokens, gathered, preferred_element_type=jnp.float32).astype(jnp.bfloat16)
    input_grad = lax.psum_scatter(
        lax.dot_general(
            key_cotangent, gathered, (((1,), (1,)), ((), ())), preferred_element_type=jnp.float32
        ).astype(jnp.bfloat16),
        "tensor",
        scatter_dimension=0,
        tiled=True,
    )
    weight_grad = lax.psum_scatter(
        lax.dot_general(
            tokens, key_cotangent, (((0,), (0,)), ((), ())), preferred_element_type=jnp.float32
        ).astype(jnp.bfloat16),
        "fsdp",
        scatter_dimension=0,
        tiled=True,
    )
    own_frag = local_frag[0]
    islands = lax.axis_size("island")
    part_sum = lax.psum_scatter(own_frag, "island", scatter_dimension=1, tiled=True).astype(
        jnp.float32
    )
    share_rows = part_sum.shape[1]
    first_share = lax.axis_index("island") * share_rows
    outer_part = lax.dynamic_slice_in_dim(outer_frag, first_share, share_rows, 1)
    moment_part = lax.dynamic_slice_in_dim(momentum, first_share, share_rows, 1)
    average = outer_part - part_sum / islands
    moment_next = beta_outer * moment_part + average
    outer_next = outer_part - outer_rate * (average + beta_outer * moment_next)
    new_outer, new_momentum = (
        lax.all_gather(outer_next.astype(jnp.bfloat16), "island", axis=1, tiled=True).astype(
            outer_next.dtype
        ),
        lax.all_gather(moment_next.astype(jnp.bfloat16), "island", axis=1, tiled=True).astype(
            moment_next.dtype
        ),
    )
    return (keys, input_grad, weight_grad[None], new_outer, new_momentum)


def solution(mesh):
    return jax.shard_map(
        body,
        mesh=mesh,
        in_specs=(
            P(("island", "fsdp"), None),
            P("island", "fsdp", "tensor"),
            P(("island", "fsdp"), "tensor"),
            P("island", None, "fsdp", "tensor"),
            P(None, "fsdp", "tensor"),
            P(None, "fsdp", "tensor"),
        ),
        out_specs=(
            P(("island", "fsdp"), "tensor"),
            P(("island", "fsdp", "tensor"), None),
            P("island", "fsdp", "tensor"),
            P(None, "fsdp", "tensor"),
            P(None, "fsdp", "tensor"),
        ),
        check_vma=False,
    )
```

profile of v0, /device:TPU:1, one launch (start us, length us, event | category | flops | bytes accessed | tf_op | source)
XLA Modules:
  0.0 521.4 jit_solution(2583883865695155933)
XLA Ops:
  8.0 0.0 reduce-scatter.8.cloned.1.call-start
  8.1 0.7 reduce-scatter.8.cloned.1.call-update
  8.7 0.0 all-gather.9.cloned.1.call-start
  8.8 0.5 all-gather.9.cloned.1.call-update
  9.3 0.0 all-gather.5.cloned.1.call-start
  9.4 218.6 %reduce-scatter.8.cloned.1.call-done = bf16[2,32,512]{2,1,0:T(8,128)(2,1)} async-done(((bf16[2,512,512]{2,1,0:T(8,128)(2,1)}), bf16[2,32,512]{2,1,0:T(8,128)(2,1)}) %reduce-scatter.8.cloned.1.call-update) | async-done | bytes 65552 | tf_op jit(solution)/shard_map/reduce_scatter | solution.py:32
  227.9 1.7 fusion.6
  229.6 0.0 all-gather.5.cloned.1.call-update
  229.7 0.0 all-gather.7.cloned.1.call-start
  229.7 0.5 all-gather.7.cloned.1.call-update
  230.2 0.0 reduce-scatter.6.cloned.1.call-start
  230.3 3.5 convolution_convert_fusion
  233.8 0.0 reduce-scatter.6.cloned.1.call-update
  233.8 0.0 reduce-scatter.4.cloned.1.call-start
  233.9 0.0 all-gather.9.cloned.1.call-done
  233.9 0.7 copy-done.2
  234.7 4.2 convolution_convert_fusion.1
  238.9 79.6 %all-gather.5.cloned.1.call-done = bf16[2,512,512]{2,1,0:T(8,128)(2,1)} async-done(((bf16[2,32,512]{2,1,0:T(8,128)(2,1)}), bf16[2,512,512]{2,1,0:T(8,128)(2,1)}) %all-gather.5.cloned.1.call-update) | async-done | bytes 1048592 | tf_op jit(solution)/shard_map/all_gather | solution.py:43
  318.5 2.8 convert_element_type.29
  321.3 87.7 %all-gather.7.cloned.1.call-done = bf16[2,512,512]{2,1,0:T(8,128)(2,1)} async-done(((bf16[2,32,512]{2,1,0:T(8,128)(2,1)}), bf16[2,512,512]{2,1,0:T(8,128)(2,1)}) %all-gather.7.cloned.1.call-update) | async-done | bytes 1048592 | tf_op jit(solution)/shard_map/all_gather | solution.py:46
  409.1 3.0 convert_element_type.31
  412.0 1.2 fusion.3
  413.3 58.8 %reduce-scatter.6.cloned.1.call-done = bf16[512,256]{1,0:T(8,128)(2,1)} async-done(((bf16[6144,256]{1,0:T(8,128)(2,1)}), bf16[512,256]{1,0:T(8,128)(2,1)}) %reduce-scatter.6.cloned.1.call-update) | async-done | bytes 262160 | tf_op jit(solution)/shard_map/reduce_scatter | solution.py:22
  472.0 41.7 %reduce-scatter.4.cloned.1.call-done = bf16[32,6144]{1,0:T(8,128)(2,1)} async-done(((bf16[128,6144]{1,0:T(8,128)(2,1)}), bf16[32,6144]{1,0:T(8,128)(2,1)}) %reduce-scatter.4.cloned.1.call-update) | async-done | bytes 393232 | tf_op jit(solution)/shard_map/reduce_scatter | solution.py:14
  (6 shorter events, 0.0 us)
Async XLA Ops:
  8.0 222.3 %copy-start = (bf16[128,6144]{1,0:T(8,128)(2,1)S(1)}, bf16[128,6144]{1,0:T(8,128)(2,1)}, u32[]{:S(2)}) copy-start(bf16[128,6144]{1,0:T(8,128)(2,1)} %param.6) | copy-start | bytes 4718596
  8.0 219.9 %reduce-scatter.8.cloned.1.call-start = ((), (), s32[]{:S(2)}) async-start(), calls=%async_computation.5 | async-start | bytes 1114112 | tf_op jit(solution)/shard_map/reduce_scatter | solution.py:32
  8.7 225.2 %all-gather.9.cloned.1.call-start = ((), (), s32[]{:S(2)}) async-start(), calls=%async_computation.8 | async-start | bytes 3407872 | tf_op jit(solution)/shard_map/all_gather | solution.py:12
  9.3 309.2 %all-gather.5.cloned.1.call-start = ((), (), s32[]{:S(2)}) async-start(), calls=%async_computation.6 | async-start | bytes 1114112 | tf_op jit(solution)/shard_map/all_gather | solution.py:43
  229.7 179.4 %all-gather.7.cloned.1.call-start = ((), (), s32[]{:S(2)}) async-start(), calls=%async_computation.7 | async-start | bytes 1114112 | tf_op jit(solution)/shard_map/all_gather | solution.py:46
  230.2 241.8 %reduce-scatter.6.cloned.1.call-start = ((), (), s32[]{:S(2)}) async-start(), calls=%async_computation.4 | async-start | bytes 3407872 | tf_op jit(solution)/shard_map/reduce_scatter | solution.py:22
  233.8 0.8 copy-start.2
  233.8 279.9 %reduce-scatter.4.cloned.1.call-start = ((), (), s32[]{:S(2)}) async-start(), calls=%async_computation.3 | async-start | bytes 1966080 | tf_op jit(solution)/shard_map/reduce_scatter | solution.py:14
  409.1 3.0 copy-start.1
Sparse Core Ops, SparseCore 0:
  13.8 214.0 reduce-scatter.7
Sparse Core Ops, SparseCore 1:
  11.6 64.6 all-gather.8
  229.7 88.7 all-gather.4
  322.7 86.3 all-gather.6
  412.8 59.2 reduce-scatter.5
  475.8 38.0 reduce-scatter.3
where the time goes:
time: 522 us; the launch traced here: 521 us
  waiting for transfers between devices  488 us (93%)
  between operations  15.7 us (3%)
  matrix products  8.92 us (2%)
  other arithmetic  7.52 us (1%)
    reduce_scatter x1, waiting for transfers between devices, body(): lax.psum_scatter(own_frag, 'island', scatter_dimension=1, tiled=True)  219 us
    all_gather x1, waiting for transfers between devices, body(): lax.all_gather(moment_next.astype(jnp.bfloat16), 'island', axis=1, tiled=...  87.7 us
    all_gather x1, waiting for transfers between devices, body(): lax.all_gather(outer_next.astype(jnp.bfloat16), 'island', axis=1, tiled=T...  79.6 us
    reduce_scatter x1, waiting for transfers between devices, body(): lax.psum_scatter(lax.dot_general(tokens, key_cotangent, (((0,), (0,)), ((...  58.8 us
    reduce_scatter x1, waiting for transfers between devices, body(): lax.psum_scatter(lax.dot_general(key_cotangent, gathered, (((1,), (1,)),...  41.7 us
  transfers between devices with their start and end apart: 6, of which 5 were waited for; matrix products, arithmetic and copies ran while one was open for 3% of the time, Pallas kernels for 0%

commit v1 on v0

v1 whole, which is shorter than its diff:
```python
import jax
import jax.numpy as jnp
from jax import lax
from jax.experimental import pallas as pl
from jax.experimental.pallas import tpu as pltpu
from jax.sharding import PartitionSpec as P

outer_rate = 0.7
beta_outer = 0.9
MESH = pl.DeviceIdType.MESH
F, T, Y = 12, 4, 8
QR, DB, KT = 32, 512, 256
AGP, AGM = 6, 5
RSP, RSM = 5, 6
YP = (4, 3)
YM = (3, 4)
bf16, f32 = jnp.bfloat16, jnp.float32


def kernel(tok, w, cot, frag, outer, mom, keys_o, dx_o, dw_o, no_o, nm_o,
           xa, ca, wg, dxs, kp, ksp, ksm, krp, krm, kfin, dwp, dwr, dws, dwx, dwf,
           fr, yss, yrr, ys, xr, sm, ov, mv, nov, nmv,
           lsem, tks, tkr, cts, ctr, wss, wsr, ags, agr, dxsm, dxr, kss, ksr, kts, ktr,
           dwss, dwsr, yrs, yrrs, xss, xsr, yas, yar, osem):
    isl = lax.axis_index("island")
    f = lax.axis_index("fsdp")
    t = lax.axis_index("tensor")
    y = lax.rem(isl, Y)
    xh = isl - y
    fz = lambda k: lax.rem(f + (k + F), F)
    ty = lambda k: lax.rem(t + (k + T), T)
    yy = lambda k: lax.rem(y + (k + 2 * Y), Y)
    yd = lambda k: {"island": xh + yy(k)}
    xpart = {"island": lax.rem(isl + Y, 2 * Y)}
    core = lax.rem(t, 2)
    xlo = lax.div(t, 2)
    tc = t + 1 - 2 * core
    tx = ty(2)
    pending = []

    def local(src, dst, sem):
        c = pltpu.make_async_copy(src, dst, sem)
        c.start()
        return c

    def rc(src, dst, ss, rs, dev):
        return pltpu.make_async_remote_copy(src_ref=src, dst_ref=dst, send_sem=ss, recv_sem=rs,
                                            device_id=dev, device_id_type=MESH)

    def send(*a):
        c = rc(*a)
        c.start()
        pending.append(c)

    def got(dst, rs, ss, dev):
        rc(dst, dst, ss, rs, dev).wait_recv()

    cot_rows = lambda q: cot.at[pl.ds(pl.multiple_of(q * QR, QR), QR), :]
    tok_blk = lambda b: tok.at[pl.ds(pl.multiple_of(t * QR, QR), QR), pl.ds(pl.multiple_of(b * DB, DB), DB)]
    dx_blk = lambda b: dx_o.at[:, pl.ds(pl.multiple_of(b * DB, DB), DB)]

    bar = pltpu.get_barrier_semaphore()
    peers = [{"fsdp": fz(k)} for k in range(1, F)] + [{"tensor": ty(k)} for k in range(1, T)]
    peers += [yd(1), yd(-1), xpart]
    for d in peers:
        pl.semaphore_signal(bar, inc=1, device_id=d, device_id_type=MESH)

    l_w = local(w, wg.at[t], lsem.at[0])
    l_c = local(cot_rows(t), ca.at[f, t], lsem.at[1])
    l_x = local(tok_blk(f), xa.at[f], lsem.at[2])
    l_f = local(frag, fr, lsem.at[3])
    pl.semaphore_wait(bar, len(peers))

    for j in range(1, T):
        send(cot_rows(ty(j)), ca.at[f, t], cts.at[j - 1], ctr.at[j - 1], {"tensor": ty(j)})
    for h in range(2):
        send(frag.at[yy(YP[h]), h], yrr.at[0, h, 0], yrs.at[0, h, 0], yrrs.at[0, h, 0], yd(1))
        send(frag.at[yy(-YM[h]), h], yrr.at[1, h, 0], yrs.at[1, h, 0], yrrs.at[1, h, 0], yd(-1))
    send(w, wg.at[t], wss.at[0], wsr.at[0], {"tensor": tx})
    send(w, wg.at[t], wss.at[1], wsr.at[1], {"tensor": tc})
    for k in (6, 5, -5, 4, -4, 3, -3, 2, -2, 1, -1):
        b = fz(k)
        i = k % F - 1
        send(tok_blk(b), xa.at[f], tks.at[i], tkr.at[i], {"fsdp": b})
    l_o = local(outer, ov, lsem.at[4])
    l_m = local(mom, mv, lsem.at[5])

    l_c.wait()
    for j in range(1, T):
        got(ca.at[f, ty(-j)], ctr.at[j - 1], cts.at[j - 1], {"tensor": ty(-j)})

    def ag_send(s):
        if s < AGP:
            b = fz(-s)
            send(ca.at[b], ca.at[b], ags.at[0, s], agr.at[0, s], {"fsdp": fz(1)})
        if s < AGM:
            b = fz(s)
            send(ca.at[b], ca.at[b], ags.at[1, s], agr.at[1, s], {"fsdp": fz(-1)})

    def ag_step(s):
        if s <= AGP:
            got(ca.at[fz(-s)], agr.at[0, s - 1], ags.at[0, s - 1], {"fsdp": fz(-1)})
        if s <= AGM:
            got(ca.at[fz(s)], agr.at[1, s - 1], ags.at[1, s - 1], {"fsdp": fz(1)})
        ag_send(s)

    def dx_step(s):
        ks = [k for k, ok in ((-s, s <= AGP), (s, s <= AGM and s > 0)) if ok]
        bs = [fz(k) for k in ks]
        acc = None
        for q in range(T):
            lhs = jnp.concatenate([ca[b, q] for b in bs], axis=0) if len(bs) > 1 else ca[bs[0], q]
            p = lax.dot_general(lhs, wg[q], (((1,), (1,)), ((), ())), preferred_element_type=f32)
            acc = p if acc is None else acc + p
        for n, (k, b) in enumerate(zip(ks, bs)):
            dxs[b] = acc[n * QR:(n + 1) * QR].astype(bf16)
            if k != 0:
                i = k % F - 1
                send(dxs.at[b], dx_blk(f), dxsm.at[i], dxr.at[i], {"fsdp": b})
        if s == 0:
            pending_local.append(local(dxs.at[f], dx_blk(f), osem.at[0]))

    pending_local = []

    def y_step(s):
        for h in range(2):
            for d, hops, sgn in ((0, YP[h], 1), (1, YM[h], -1)):
                if s < hops:
                    got(yrr.at[d, h, s - 1], yrrs.at[d, h, s - 1], yrs.at[d, h, s - 1], yd(-sgn))
                    b = yy(sgn * (hops - s))
                    yss[d, h, s - 1] = (yrr[d, h, s - 1].astype(f32) + fr[b, h].astype(f32)).astype(bf16)
                    send(yss.at[d, h, s - 1], yrr.at[d, h, s], yrs.at[d, h, s], yrrs.at[d, h, s], yd(sgn))

    def y_last():
        for h in range(2):
            got(yrr.at[0, h, YP[h] - 1], yrrs.at[0, h, YP[h] - 1], yrs.at[0, h, YP[h] - 1], yd(-1))
            got(yrr.at[1, h, YM[h] - 1], yrrs.at[1, h, YM[h] - 1], yrs.at[1, h, YM[h] - 1], yd(1))
            ys[h] = (yrr[0, h, YP[h] - 1].astype(f32) + yrr[1, h, YM[h] - 1].astype(f32)
                     + fr[y, h].astype(f32)).astype(bf16)
            send(ys.at[h], xr.at[h], xss.at[h], xsr.at[h], xpart)

    def update(b, h):
        avg = ov[b, h] - sm[b, h].astype(f32) * (1.0 / (2 * Y))
        nm = beta_outer * mv[b, h] + avg
        nmv[b, h] = nm
        nov[b, h] = ov[b, h] - outer_rate * (avg + beta_outer * nm)

    def ya_send(s):
        for h in range(2):
            if s < YP[h]:
                b = yy(-s)
                send(sm.at[b, h], sm.at[b, h], yas.at[0, h, s], yar.at[0, h, s], yd(1))
            if s < YM[h]:
                b = yy(s)
                send(sm.at[b, h], sm.at[b, h], yas.at[1, h, s], yar.at[1, h, s], yd(-1))

    def ya_first():
        for h in range(2):
            got(xr.at[h], xsr.at[h], xss.at[h], xpart)
            sm[y, h] = (ys[h].astype(f32) + xr[h].astype(f32)).astype(bf16)
        ya_send(0)

    def ya_step(s):
        done = []
        for h in range(2):
            if s <= YP[h]:
                b = yy(-s)
                got(sm.at[b, h], yar.at[0, h, s - 1], yas.at[0, h, s - 1], yd(-1))
                done.append((b, h))
            if s <= YM[h]:
                b = yy(s)
                got(sm.at[b, h], yar.at[1, h, s - 1], yas.at[1, h, s - 1], yd(1))
                done.append((b, h))
        ya_send(s)
        for b, h in done:
            update(b, h)

    def k_all():
        l_x.wait()
        for k in range(1, F):
            got(xa.at[fz(-k)], tkr.at[k - 1], tks.at[k - 1], {"fsdp": fz(-k)})

        def one(q, c):
            r = jnp.dot(xa[...].reshape(F * QR, DB), wg[q], preferred_element_type=f32)
            kp[q] = r.reshape(F, QR, KT)
            return c
        lax.fori_loop(0, T, one, 0)

    def k_step(s):
        for d, hops, sgn, rv, sd in ((0, RSP, 1, krp, ksp), (1, RSM, -1, krm, ksm)):
            if s < hops:
                b = fz(sgn * (hops - s))
                v = kp[:, b]
                if s > 0:
                    got(rv.at[s - 1], ksr.at[d, s - 1], kss.at[d, s - 1], {"fsdp": fz(-sgn)})
                    v = v + rv[s - 1].astype(f32)
                sd[s] = v.astype(bf16)
                send(sd.at[s], rv.at[s], kss.at[d, s], ksr.at[d, s], {"fsdp": fz(sgn)})

    def k_last():
        got(krp.at[RSP - 1], ksr.at[0, RSP - 1], kss.at[0, RSP - 1], {"fsdp": fz(-1)})
        got(krm.at[RSM - 1], ksr.at[1, RSM - 1], kss.at[1, RSM - 1], {"fsdp": fz(1)})
        kfin[...] = (kp[:, f] + krp[RSP - 1].astype(f32) + krm[RSM - 1].astype(f32)).astype(bf16)
        mine = keys_o.at[pl.ds(pl.multiple_of(t * QR, QR), QR), :]
        for j in range(1, T):
            q = ty(j)
            send(kfin.at[q], mine, kts.at[j - 1], ktr.at[j - 1], {"tensor": q})
        pending_local.append(local(kfin.at[t], mine, osem.at[1]))

    def w_all():
        def one(q, c):
            r = lax.dot_general(xa[...].reshape(F * QR, DB), ca[:, q].reshape(F * QR, KT),
                                (((0,), (0,)), ((), ())), preferred_element_type=f32)
            dwp[q] = r.astype(bf16)
            return c
        lax.fori_loop(0, T, one, 0)
        for m in range(2):
            send(dwp.at[2 * m + 1 - core], dwr.at[m], dwss.at[m], dwsr.at[m], {"tensor": tc})

    def w_mid():
        for m in range(2):
            got(dwr.at[m], dwsr.at[m], dwss.at[m], {"tensor": tc})
        o = 1 - xlo
        dws[...] = (dwp[2 * o + core].astype(f32) + dwr[o].astype(f32)).astype(bf16)
        send(dws, dwx, dwss.at[2], dwsr.at[2], {"tensor": tx})

    def w_last():
        got(dwx, dwsr.at[2], dwss.at[2], {"tensor": tx})
        dwf[...] = (dwp[2 * xlo + core].astype(f32) + dwr[xlo].astype(f32) + dwx[...].astype(f32)).astype(bf16)
        pending_local.append(local(dwf, dw_o, osem.at[2]))

    ag_send(0)
    l_f.wait()
    y_step(1)
    ag_step(1)
    got(wg.at[tx], wsr.at[0], wss.at[0], {"tensor": tx})
    send(wg.at[tx], wg.at[tx], wss.at[2], wsr.at[2], {"tensor": tc})
    y_step(2)
    ag_step(2)
    l_w.wait()
    got(wg.at[tc], wsr.at[1], wss.at[1], {"tensor": tc})
    txc = lax.rem(tc + 2, T)
    got(wg.at[txc], wsr.at[2], wss.at[2], {"tensor": tc})
    dx_step(2)
    dx_step(1)
    y_step(3)
    ag_step(3)
    dx_step(3)
    dx_step(0)
    y_last()
    ag_step(4)
    dx_step(4)
    ya_first()
    k_all()
    k_step(0)
    ag_step(5)
    dx_step(5)
    k_step(1)
    l_o.wait()
    l_m.wait()
    ya_step(1)
    update(y, 0)
    update(y, 1)
    ag_step(6)
    dx_step(6)
    k_step(2)
    ya_step(2)
    w_all()
    k_step(3)
    ya_step(3)
    w_mid()
    k_step(4)
    ya_step(4)
    pending_local.append(local(nov, no_o, osem.at[3]))
    pending_local.append(local(nmv, nm_o, osem.at[4]))
    k_step(5)
    w_last()
    k_last()
    for k in range(1, F):
        got(dx_blk(fz(-k)), dxr.at[k - 1], dxsm.at[k - 1], {"fsdp": fz(-k)})
    for j in range(1, T):
        q = ty(-j)
        got(keys_o.at[pl.ds(pl.multiple_of(q * QR, QR), QR), :], ktr.at[j - 1], kts.at[j - 1], {"tensor": q})
    for c in pending_local:
        c.wait()
    for c in pending:
        c.wait_send()


def body(tokens, key_weight, key_cotangent, local_frag, outer_frag, momentum):
    FS = (Y, 2, 64, 512)
    V, DMA = pltpu.VMEM, pltpu.SemaphoreType.DMA
    blk = (T, QR, KT)
    any_ = pl.BlockSpec(memory_space=pl.ANY)
    keys, dx, dw, no, nm = pl.pallas_call(
        kernel,
        out_shape=(
            jax.ShapeDtypeStruct((T * QR, KT), bf16),
            jax.ShapeDtypeStruct((QR, F * DB), bf16),
            jax.ShapeDtypeStruct((DB, KT), bf16),
            jax.ShapeDtypeStruct(FS, f32),
            jax.ShapeDtypeStruct(FS, f32),
        ),
        in_specs=[any_] * 6,
        out_specs=(any_,) * 5,
        scratch_shapes=[
            V((F, QR, DB), bf16), V((F,) + blk, bf16), V((T, DB, KT), bf16), V((F, QR, DB), bf16),
            V((T, F, QR, KT), f32), V((RSP,) + blk, bf16), V((RSM,) + blk, bf16),
            V((RSP,) + blk, bf16), V((RSM,) + blk, bf16), V(blk, bf16),
            V((T, DB, KT), bf16), V((2, DB, KT), bf16), V((DB, KT), bf16), V((DB, KT), bf16), V((DB, KT), bf16),
            V(FS, bf16), V((2, 2, 3, 64, 512), bf16), V((2, 2, 4, 64, 512), bf16),
            V((2, 64, 512), bf16), V((2, 64, 512), bf16), V(FS, bf16),
            V(FS, f32), V(FS, f32), V(FS, f32), V(FS, f32),
            DMA((6,)), DMA((11,)), DMA((11,)), DMA((3,)), DMA((3,)), DMA((3,)), DMA((3,)),
            DMA((2, 6)), DMA((2, 6)), DMA((11,)), DMA((11,)), DMA((2, 6)), DMA((2, 6)), DMA((3,)), DMA((3,)),
            DMA((3,)), DMA((3,)), DMA((2, 2, 4)), DMA((2, 2, 4)), DMA((2,)), DMA((2,)),
            DMA((2, 2, 4)), DMA((2, 2, 4)), DMA((5,)),
        ],
        compiler_params=pltpu.CompilerParams(collective_id=0, has_side_effects=True,
                                             vmem_limit_bytes=48 << 20),
    )(tokens, key_weight[0], key_cotangent, local_frag.reshape(FS), outer_frag.reshape(FS), momentum.reshape(FS))
    return keys, dx, dw[None], no.reshape(outer_frag.shape), nm.reshape(momentum.shape)


def solution(mesh):
    return jax.shard_map(
        body,
        mesh=mesh,
        in_specs=(
            P(("island", "fsdp"), None),
            P("island", "fsdp", "tensor"),
            P(("island", "fsdp"), "tensor"),
            P("island", None, "fsdp", "tensor"),
            P(None, "fsdp", "tensor"),
            P(None, "fsdp", "tensor"),
        ),
        out_specs=(
            P(("island", "fsdp"), "tensor"),
            P(("island", "fsdp", "tensor"), None),
            P("island", "fsdp", "tensor"),
            P(None, "fsdp", "tensor"),
            P(None, "fsdp", "tensor"),
        ),
        check_vma=False,
    )
```

time: 522 us -> 91.1 us (0.17)
  waiting for transfers between devices: 488 us -> 0 us
  Pallas kernels: 0 us -> 78.8 us
  between operations: 15.7 us -> 0.66 us
  local copies, waits for them, and re-layouts: 0.74 us -> 10.2 us
  matrix products: 8.92 us -> 0 us
  other arithmetic: 7.52 us -> 0 us
    reduce_scatter x3 -> x0, waiting for transfers between devices: 319 us -> none  [the longest x1 219 us: body(): lax.psum_scatter(own_frag, 'island', scatter_dimension=1, tiled=True)]
    all_gather x3 -> x0, waiting for transfers between devices: 167 us -> none  [the longest x1 87.7 us: body(): lax.all_gather(moment_next.astype(jnp.bfloat16), 'island', axis=1, tiled=...]
    pallas_call x0 -> x1, Pallas kernels: none -> 78.8 us  [body(): pl.pallas_call(kernel, out_shape=(jax.ShapeDtypeStruct((T * QR, KT), bf16...]
    unnamed x6 -> x15, local copies, waits for them, and re-layouts: 0.74 us -> 10.2 us
    dot_general x3 -> x0, matrix products: 8.92 us -> none  [the longest x1 4.18 us: body(): lax.dot_general(key_cotangent, gathered, (((1,), (1,)), ((), ())), prefer...]
    convert_element_type x3 -> x0, other arithmetic: 7.52 us -> none  [the longest x1 2.98 us: body(): lax.all_gather(moment_next.astype(jnp.bfloat16), 'island', axis=1, tiled=...]
  transfers between devices with their start and end apart: 6 -> 0, of which waited for: 5 -> 0; matrix products, arithmetic and copies ran while one was open for 3% -> 0% of each run, Pallas kernels for 0% -> 0%
where the time goes in v1:
time: 91.1 us; the launch traced here: 89.6 us
  Pallas kernels  78.8 us (86%)
  local copies, waits for them, and re-layouts  10.2 us (11%)
    pallas_call x1, Pallas kernels, body(): pl.pallas_call(kernel, out_shape=(jax.ShapeDtypeStruct((T * QR, KT), bf16...  78.8 us
    unnamed x15, local copies, waits for them, and re-layouts  10.2 us

profile of v1, /device:TPU:1, one launch (start us, length us, event | category | flops | bytes accessed | tf_op | source)
XLA Modules:
  0.0 89.6 jit_solution(5207635048087897015)
XLA Ops:
  0.6 0.0 copy-start
  0.6 1.4 %copy-done = bf16[128,6144]{1,0:T(8,128)(2,1)S(1)} copy-done((bf16[128,6144]{1,0:T(8,128)(2,1)S(1)}, bf16[128,6144]{1,0:T(8,128)(2,1)}, u32[]{:S(2)}) %copy-start) | copy-done | bytes 1572888
  2.0 0.0 copy-start.1
  2.0 1.2 %copy-done.1 = bf16[1,2,512,512]{3,2,1,0:T(8,128)(2,1)S(1)} copy-done((bf16[1,2,512,512]{3,2,1,0:T(8,128)(2,1)S(1)}, bf16[1,2,512,512]{3,2,1,0:T(8,128)(2,1)}, u32[]{:S(2)}) %copy-start.1) | copy-done | bytes 1048600
  3.3 0.0 copy-start.2
  3.3 0.9 %copy-done.2 = bf16[1,512,256]{2,1,0:T(8,128)(2,1)S(1)} copy-done((bf16[1,512,256]{2,1,0:T(8,128)(2,1)S(1)}, bf16[1,512,256]{2,1,0:T(8,128)(2,1)}, u32[]{:S(2)}) %copy-start.2) | copy-done | bytes 262168
  4.2 0.0 copy-start.3
  4.2 0.8 copy-done.3
  5.1 78.8 %shard_map.101 = (bf16[128,256]{1,0:T(8,128)(2,1)S(1)}, bf16[32,6144]{1,0:T(8,128)(2,1)S(1)}, bf16[512,256]{1,0:T(8,128)(2,1)S(1)}, f32[8,2,64,512]{3,2,1,0:T(8,128)S(1)}, f32[8,2,64,512]{3,2,1,0:T(8,128)}) custom-call(bf16[128,6144]{1,0:T(8,128)(2,1)S(1)} %copy-done, bf16[512,256]{1,0:T(8,128)(2,1)S(1)} %bitcast.9, bf16[128,256]{1,0:T(8,128)(2,1)S(1)} %copy-done.3, ...), custom_call_target="tpu_custom_call" | custom-call | tf_op jit(solution)/shard_map/pallas_call | solution.py:295
  83.9 0.6 copy.16
  84.5 0.7 copy.17
  85.2 0.7 copy.18
  85.9 0.0 copy-start.4
  85.9 1.3 %copy.19 = f32[2,512,512]{2,1,0:T(8,128)} copy(f32[2,512,512]{2,1,0:T(8,128)S(1)} %bitcast.7) | data formatting | bytes 4194304
  87.3 1.0 %copy-done.4 = f32[8,2,64,512]{3,2,1,0:T(8,128)S(1)} copy-done((f32[8,2,64,512]{3,2,1,0:T(8,128)S(1)}, f32[8,2,64,512]{3,2,1,0:T(8,128)}, u32[]{:S(2)}) %copy-start.4) | copy-done | bytes 2097176
  88.3 1.3 %copy.20 = f32[2,512,512]{2,1,0:T(8,128)} copy(f32[2,512,512]{2,1,0:T(8,128)S(1)} %bitcast.13) | data formatting | bytes 4194304
Async XLA Ops:
  0.6 1.4 %copy-start = (bf16[128,6144]{1,0:T(8,128)(2,1)S(1)}, bf16[128,6144]{1,0:T(8,128)(2,1)}, u32[]{:S(2)}) copy-start(bf16[128,6144]{1,0:T(8,128)(2,1)} %tok.1) | copy-start | bytes 4718596
  2.0 1.2 %copy-start.1 = (bf16[1,2,512,512]{3,2,1,0:T(8,128)(2,1)S(1)}, bf16[1,2,512,512]{3,2,1,0:T(8,128)(2,1)}, u32[]{:S(2)}) copy-start(bf16[1,2,512,512]{3,2,1,0:T(8,128)(2,1)} %param.9) | copy-start | bytes 3145732
  3.3 0.9 %copy-start.2 = (bf16[1,512,256]{2,1,0:T(8,128)(2,1)S(1)}, bf16[1,512,256]{2,1,0:T(8,128)(2,1)}, u32[]{:S(2)}) copy-start(bf16[1,512,256]{2,1,0:T(8,128)(2,1)} %param.7) | copy-start | bytes 786436
  4.2 0.8 copy-start.3
  85.9 2.3 %copy-start.4 = (f32[8,2,64,512]{3,2,1,0:T(8,128)S(1)}, f32[8,2,64,512]{3,2,1,0:T(8,128)}, u32[]{:S(2)}) copy-start(f32[8,2,64,512]{3,2,1,0:T(8,128)} %get-tuple-element.14) | copy-start | bytes 6291460

commit v2 on v1

--- a/solution.py
+++ b/solution.py
@@ -18,10 +18,10 @@
 
 
 def kernel(tok, w, cot, frag, outer, mom, keys_o, dx_o, dw_o, no_o, nm_o,
-           xa, ca, wg, dxs, kp, ksp, ksm, krp, krm, kfin, dwp, dwr, dws, dwx, dwf,
-           fr, yss, yrr, ys, xr, sm, ov, mv, nov, nmv,
+           xa, ca, wg, dxs, kp, ksp, ksm, krp, krm, kfin, dwp, dwr, dws, dwx,
+           fr, yss, yrr, ys, xr, sm, ov, mv,
            lsem, tks, tkr, cts, ctr, wss, wsr, ags, agr, dxsm, dxr, kss, ksr, kts, ktr,
-           dwss, dwsr, yrs, yrrs, xss, xsr, yas, yar, osem):
+           dwss, dwsr, yrs, yrrs, xss, xsr, yas, yar):
     isl = lax.axis_index("island")
     f = lax.axis_index("fsdp")
     t = lax.axis_index("tensor")
@@ -78,10 +78,13 @@
         send(frag.at[yy(-YM[h]), h], yrr.at[1, h, 0], yrs.at[1, h, 0], yrrs.at[1, h, 0], yd(-1))
     send(w, wg.at[t], wss.at[0], wsr.at[0], {"tensor": tx})
     send(w, wg.at[t], wss.at[1], wsr.at[1], {"tensor": tc})
-    for k in (6, 5, -5, 4, -4, 3, -3, 2, -2, 1, -1):
-        b = fz(k)
-        i = k % F - 1
-        send(tok_blk(b), xa.at[f], tks.at[i], tkr.at[i], {"fsdp": b})
+    def tok_send(ks):
+        for k in ks:
+            b = fz(k)
+            i = k % F - 1
+            send(tok_blk(b), xa.at[f], tks.at[i], tkr.at[i], {"fsdp": b})
+
+    tok_send((6, 5, -5))
     l_o = local(outer, ov, lsem.at[4])
     l_m = local(mom, mv, lsem.at[5])
 
@@ -113,14 +116,13 @@
             p = lax.dot_general(lhs, wg[q], (((1,), (1,)), ((), ())), preferred_element_type=f32)
             acc = p if acc is None else acc + p
         for n, (k, b) in enumerate(zip(ks, bs)):
-            dxs[b] = acc[n * QR:(n + 1) * QR].astype(bf16)
-            if k != 0:
+            r = acc[n * QR:(n + 1) * QR].astype(bf16)
+            if k == 0:
+                dx_o[:, pl.ds(pl.multiple_of(f * DB, DB), DB)] = r
+            else:
                 i = k % F - 1
+                dxs[b] = r
                 send(dxs.at[b], dx_blk(f), dxsm.at[i], dxr.at[i], {"fsdp": b})
-        if s == 0:
-            pending_local.append(local(dxs.at[f], dx_blk(f), osem.at[0]))
-
-    pending_local = []
 
     def y_step(s):
         for h in range(2):
@@ -142,8 +144,8 @@
     def update(b, h):
         avg = ov[b, h] - sm[b, h].astype(f32) * (1.0 / (2 * Y))
         nm = beta_outer * mv[b, h] + avg
-        nmv[b, h] = nm
-        nov[b, h] = ov[b, h] - outer_rate * (avg + beta_outer * nm)
+        nm_o[b, h] = nm
+        no_o[b, h] = ov[b, h] - outer_rate * (avg + beta_outer * nm)
 
     def ya_send(s):
         for h in range(2):
@@ -160,31 +162,37 @@
             sm[y, h] = (ys[h].astype(f32) + xr[h].astype(f32)).astype(bf16)
         ya_send(0)
 
+    def upd(s):
+        for h in range(2):
+            if s <= YP[h]:
+                update(yy(-s), h)
+            if 0 < s <= YM[h]:
+                update(yy(s), h)
+
     def ya_step(s):
-        done = []
         for h in range(2):
             if s <= YP[h]:
                 b = yy(-s)
                 got(sm.at[b, h], yar.at[0, h, s - 1], yas.at[0, h, s - 1], yd(-1))
-                done.append((b, h))
             if s <= YM[h]:
                 b = yy(s)
                 got(sm.at[b, h], yar.at[1, h, s - 1], yas.at[1, h, s - 1], yd(1))
-                done.append((b, h))
         ya_send(s)
-        for b, h in done:
-            update(b, h)
-
-    def k_all():
-        l_x.wait()
-        for k in range(1, F):
-            got(xa.at[fz(-k)], tkr.at[k - 1], tks.at[k - 1], {"fsdp": fz(-k)})
-
-        def one(q, c):
-            r = jnp.dot(xa[...].reshape(F * QR, DB), wg[q], preferred_element_type=f32)
-            kp[q] = r.reshape(F, QR, KT)
-            return c
-        lax.fori_loop(0, T, one, 0)
+
+    def k_make(s):
+        ks = [k for k, ok in ((RSP - s, s <= RSP), (s - RSM, s < RSM)) if ok]
+        for k in ks:
+            if k == 0:
+                l_x.wait()
+            else:
+                i = (-k) % F - 1
+                got(xa.at[fz(k)], tkr.at[i], tks.at[i], {"fsdp": fz(k)})
+        bs = [fz(k) for k in ks]
+        lhs = jnp.concatenate([xa[b] for b in bs], axis=0) if len(bs) > 1 else xa[bs[0]]
+        for q in range(T):
+            r = jnp.dot(lhs, wg[q], preferred_element_type=f32)
+            for n, b in enumerate(bs):
+                kp[q, b] = r[n * QR:(n + 1) * QR]
 
     def k_step(s):
         for d, hops, sgn, rv, sd in ((0, RSP, 1, krp, ksp), (1, RSM, -1, krm, ksm)):
@@ -201,11 +209,12 @@
         got(krp.at[RSP - 1], ksr.at[0, RSP - 1], kss.at[0, RSP - 1], {"fsdp": fz(-1)})
         got(krm.at[RSM - 1], ksr.at[1, RSM - 1], kss.at[1, RSM - 1], {"fsdp": fz(1)})
         kfin[...] = (kp[:, f] + krp[RSP - 1].astype(f32) + krm[RSM - 1].astype(f32)).astype(bf16)
-        mine = keys_o.at[pl.ds(pl.multiple_of(t * QR, QR), QR), :]
+        rows = pl.ds(pl.multiple_of(t * QR, QR), QR)
+        mine = keys_o.at[rows, :]
         for j in range(1, T):
             q = ty(j)
             send(kfin.at[q], mine, kts.at[j - 1], ktr.at[j - 1], {"tensor": q})
-        pending_local.append(local(kfin.at[t], mine, osem.at[1]))
+        keys_o[rows, :] = kfin[t]
 
     def w_all():
         def one(q, c):
@@ -226,99 +235,123 @@
 
     def w_last():
         got(dwx, dwsr.at[2], dwss.at[2], {"tensor": tx})
-        dwf[...] = (dwp[2 * xlo + core].astype(f32) + dwr[xlo].astype(f32) + dwx[...].astype(f32)).astype(bf16)
-        pending_local.append(local(dwf, dw_o, osem.at[2]))
+        dw_o[...] = (dwp[2 * xlo + core].astype(f32) + dwr[xlo].astype(f32) + dwx[...].astype(f32)).astype(bf16)
 
     ag_send(0)
+    tok_send((4, -4, 3, -3))
     l_f.wait()
     y_step(1)
     ag_step(1)
+    tok_send((2, -2, 1, -1))
+    y_step(2)
+    ag_step(2)
     got(wg.at[tx], wsr.at[0], wss.at[0], {"tensor": tx})
     send(wg.at[tx], wg.at[tx], wss.at[2], wsr.at[2], {"tensor": tc})
-    y_step(2)
-    ag_step(2)
     l_w.wait()
     got(wg.at[tc], wsr.at[1], wss.at[1], {"tensor": tc})
     txc = lax.rem(tc + 2, T)
     got(wg.at[txc], wsr.at[2], wss.at[2], {"tensor": tc})
-    dx_step(2)
+    k_make(0)
+    k_step(0)
     dx_step(1)
     y_step(3)
     ag_step(3)
-    dx_step(3)
-    dx_step(0)
+    k_make(1)
+    k_step(1)
+    dx_step(2)
     y_last()
     ag_step(4)
+    k_make(2)
+    k_step(2)
+    dx_step(3)
+    ya_first()
+    ag_step(5)
+    k_make(3)
+    k_step(3)
     dx_step(4)
-    ya_first()
-    k_all()
-    k_step(0)
-    ag_step(5)
+    ya_step(1)
+    ag_step(6)
+    dx_step(6)
+    k_make(4)
+    k_step(4)
     dx_step(5)
-    k_step(1)
+    k_make(5)
+    k_step(5)
+    w_all()
+    ya_step(2)
+    dx_step(0)
+    w_mid()
+    ya_step(3)
+    k_last()
     l_o.wait()
     l_m.wait()
-    ya_step(1)
-    update(y, 0)
-    update(y, 1)
-    ag_step(6)
-    dx_step(6)
-    k_step(2)
-    ya_step(2)
-    w_all()
-    k_step(3)
-    ya_step(3)
-    w_mid()
-    k_step(4)
+    for s in range(4):
+        upd(s)
     ya_step(4)
-    pending_local.append(local(nov, no_o, osem.at[3]))
-    pending_local.append(local(nmv, nm_o, osem.at[4]))
-    k_step(5)
+    upd(4)
     w_last()
-    k_last()
     for k in range(1, F):
         got(dx_blk(fz(-k)), dxr.at[k - 1], dxsm.at[k - 1], {"fsdp": fz(-k)})
     for j in range(1, T):
         q = ty(-j)
         got(keys_o.at[pl.ds(pl.multiple_of(q * QR, QR), QR), :], ktr.at[j - 1], kts.at[j - 1], {"tensor": q})
-    for c in pending_local:
-        c.wait()
     for c in pending:
         c.wait_send()
+
+
+def flush(*refs):
+    n = len(refs) // 2
+    sem = refs[-1]
+    copies = [pltpu.make_async_copy(refs[i], refs[n + i], sem.at[i]) for i in (3, 4, 1, 2, 0)]
+    for c in copies:
+        c.start()
+    for c in copies:
+        c.wait()
 
 
 def body(tokens, key_weight, key_cotangent, local_frag, outer_frag, momentum):
     FS = (Y, 2, 64, 512)
     V, DMA = pltpu.VMEM, pltpu.SemaphoreType.DMA
     blk = (T, QR, KT)
-    any_ = pl.BlockSpec(memory_space=pl.ANY)
-    keys, dx, dw, no, nm = pl.pallas_call(
+    hbm = pl.BlockSpec(memory_space=pltpu.HBM)
+    vmem = pl.BlockSpec(memory_space=pltpu.VMEM)
+    outs = (
+        jax.ShapeDtypeStruct((T * QR, KT), bf16),
+        jax.ShapeDtypeStruct((QR, F * DB), bf16),
+        jax.ShapeDtypeStruct((DB, KT), bf16),
+        jax.ShapeDtypeStruct(FS, f32),
+        jax.ShapeDtypeStruct(FS, f32),
+    )
+    fixed = lambda a: pltpu.with_memory_space_constraint(a, pltpu.HBM)
+    made = pl.pallas_call(
         kernel,
-        out_shape=(
-            jax.ShapeDtypeStruct((T * QR, KT), bf16),
-            jax.ShapeDtypeStruct((QR, F * DB), bf16),
-            jax.ShapeDtypeStruct((DB, KT), bf16),
-            jax.ShapeDtypeStruct(FS, f32),
-            jax.ShapeDtypeStruct(FS, f32),
-        ),
-        in_specs=[any_] * 6,
-        out_specs=(any_,) * 5,
+        out_shape=tuple(V(o.shape, o.dtype) for o in outs),
+        in_specs=[hbm] * 6,
+        out_specs=(vmem,) * 5,
         scratch_shapes=[
             V((F, QR, DB), bf16), V((F,) + blk, bf16), V((T, DB, KT), bf16), V((F, QR, DB), bf16),
             V((T, F, QR, KT), f32), V((RSP,) + blk, bf16), V((RSM,) + blk, bf16),
             V((RSP,) + blk, bf16), V((RSM,) + blk, bf16), V(blk, bf16),
-            V((T, DB, KT), bf16), V((2, DB, KT), bf16), V((DB, KT), bf16), V((DB, KT), bf16), V((DB, KT), bf16),
+            V((T, DB, KT), bf16), V((2, DB, KT), bf16), V((DB, KT), bf16), V((DB, KT), bf16),
             V(FS, bf16), V((2, 2, 3, 64, 512), bf16), V((2, 2, 4, 64, 512), bf16),
             V((2, 64, 512), bf16), V((2, 64, 512), bf16), V(FS, bf16),
-            V(FS, f32), V(FS, f32), V(FS, f32), V(FS, f32),
+            V(FS, f32), V(FS, f32),
             DMA((6,)), DMA((11,)), DMA((11,)), DMA((3,)), DMA((3,)), DMA((3,)), DMA((3,)),
             DMA((2, 6)), DMA((2, 6)), DMA((11,)), DMA((11,)), DMA((2, 6)), DMA((2, 6)), DMA((3,)), DMA((3,)),
             DMA((3,)), DMA((3,)), DMA((2, 2, 4)), DMA((2, 2, 4)), DMA((2,)), DMA((2,)),
-            DMA((2, 2, 4)), DMA((2, 2, 4)), DMA((5,)),
+            DMA((2, 2, 4)), DMA((2, 2, 4)),
         ],
         compiler_params=pltpu.CompilerParams(collective_id=0, has_side_effects=True,
-                                             vmem_limit_bytes=48 << 20),
-    )(tokens, key_weight[0], key_cotangent, local_frag.reshape(FS), outer_frag.reshape(FS), momentum.reshape(FS))
+                                             vmem_limit_bytes=40 << 20),
+    )(*map(fixed, (tokens, key_weight[0], key_cotangent, local_frag.reshape(FS), outer_frag.reshape(FS), momentum.reshape(FS))))
+    keys, dx, dw, no, nm = pl.pallas_call(
+        flush,
+        out_shape=outs,
+        in_specs=[vmem] * 5,
+        out_specs=(hbm,) * 5,
+        scratch_shapes=[DMA((5,))],
+        compiler_params=pltpu.CompilerParams(vmem_limit_bytes=1 << 20),
+    )(*made)
     return keys, dx, dw[None], no.reshape(outer_frag.shape), nm.reshape(momentum.shape)
 
 

time: 91.1 us -> 74.4 us (0.82)
  the two profiles are of different devices: /device:TPU:1 before, /device:TPU:29 now
where the time goes in v2:
time: 74.4 us; the launch traced here: 74.3 us
  Pallas kernels  73.6 us (99%)
    pallas_call x1, Pallas kernels, body(): pl.pallas_call(kernel, out_shape=tuple((V(o.shape, o.dtype) for o in outs...  71.4 us
    pallas_call x1, Pallas kernels, body(): pl.pallas_call(flush, out_shape=outs, in_specs=[vmem] * 5, out_specs=(hbm...  2.25 us

profile of v2, /device:TPU:29, one launch (start us, length us, event | category | flops | bytes accessed | tf_op | source)
XLA Modules:
  0.0 74.3 jit_solution(13282454655695380395)
XLA Ops:
  0.6 71.4 %shard_map.101 = (bf16[128,256]{1,0:T(8,128)(2,1)S(1)}, bf16[32,6144]{1,0:T(8,128)(2,1)S(1)}, bf16[512,256]{1,0:T(8,128)(2,1)S(1)}, f32[8,2,64,512]{3,2,1,0:T(8,128)S(1)}, f32[8,2,64,512]{3,2,1,0:T(8,128)S(1)}) custom-call(bf16[128,6144]{1,0:T(8,128)(2,1)} %tok.1, bf16[512,256]{1,0:T(8,128)(2,1)} %bitcast.10, bf16[128,256]{1,0:T(8,128)(2,1)} %cot.1, ...), custom_call_target="tpu_custom_call" | custom-call | tf_op jit(solution)/shard_map/pallas_call | solution.py:326
  72.0 2.3 %shard_map.102 = (bf16[128,256]{1,0:T(8,128)(2,1)}, bf16[32,6144]{1,0:T(8,128)(2,1)}, bf16[512,256]{1,0:T(8,128)(2,1)}, f32[8,2,64,512]{3,2,1,0:T(8,128)}, f32[8,2,64,512]{3,2,1,0:T(8,128)}) custom-call(bf16[128,256]{1,0:T(8,128)(2,1)S(1)} %get-tuple-element.15.refs_0_, bf16[32,6144]{1,0:T(8,128)(2,1)S(1)} %get-tuple-element.16.refs_1_, ...), custom_call_target="tpu_custom_call" | custom-call | tf_op jit(solution)/shard_map/pallas_call | solution.py:347

commit v3 on v2

--- a/solution.py
+++ b/solution.py
@@ -21,7 +21,7 @@
            xa, ca, wg, dxs, kp, ksp, ksm, krp, krm, kfin, dwp, dwr, dws, dwx,
            fr, yss, yrr, ys, xr, sm, ov, mv,
            lsem, tks, tkr, cts, ctr, wss, wsr, ags, agr, dxsm, dxr, kss, ksr, kts, ktr,
-           dwss, dwsr, yrs, yrrs, xss, xsr, yas, yar):
+           dwss, dwsr, yrs, yrrs, xss, xsr, yas, yar, wv):
     isl = lax.axis_index("island")
     f = lax.axis_index("fsdp")
     t = lax.axis_index("tensor")
@@ -60,7 +60,7 @@
     dx_blk = lambda b: dx_o.at[:, pl.ds(pl.multiple_of(b * DB, DB), DB)]
 
     bar = pltpu.get_barrier_semaphore()
-    peers = [{"fsdp": fz(k)} for k in range(1, F)] + [{"tensor": ty(k)} for k in range(1, T)]
+    peers = [{"fsdp": fz(1)}, {"fsdp": fz(-1)}] + [{"tensor": ty(k)} for k in range(1, T)]
     peers += [yd(1), yd(-1), xpart]
     for d in peers:
         pl.semaphore_signal(bar, inc=1, device_id=d, device_id_type=MESH)
@@ -84,7 +84,15 @@
             i = k % F - 1
             send(tok_blk(b), xa.at[f], tks.at[i], tkr.at[i], {"fsdp": b})
 
-    tok_send((6, 5, -5))
+    def wave():
+        for n in range(F // 2):
+            for d, sgn in ((0, 1), (1, -1)):
+                if n > 0:
+                    pl.semaphore_wait(wv.at[d, n - 1], 1)
+                if n < F // 2 - 1:
+                    pl.semaphore_signal(wv.at[d, n], inc=1, device_id={"fsdp": fz(sgn)}, device_id_type=MESH)
+
+    tok_send((1, -1))
     l_o = local(outer, ov, lsem.at[4])
     l_m = local(mom, mv, lsem.at[5])
 
@@ -216,33 +224,34 @@
             send(kfin.at[q], mine, kts.at[j - 1], ktr.at[j - 1], {"tensor": q})
         keys_o[rows, :] = kfin[t]
 
-    def w_all():
-        def one(q, c):
-            r = lax.dot_general(xa[...].reshape(F * QR, DB), ca[:, q].reshape(F * QR, KT),
-                                (((0,), (0,)), ((), ())), preferred_element_type=f32)
-            dwp[q] = r.astype(bf16)
-            return c
-        lax.fori_loop(0, T, one, 0)
-        for m in range(2):
-            send(dwp.at[2 * m + 1 - core], dwr.at[m], dwss.at[m], dwsr.at[m], {"tensor": tc})
+    far = 1 - xlo
+
+    def w_one(q):
+        r = lax.dot_general(xa[...].reshape(F * QR, DB), ca[:, q].reshape(F * QR, KT),
+                            (((0,), (0,)), ((), ())), preferred_element_type=f32)
+        dwp[q] = r.astype(bf16)
+
+    def w_pair(m, i):
+        w_one(2 * m + 1 - core)
+        send(dwp.at[2 * m + 1 - core], dwr.at[i], dwss.at[i], dwsr.at[i], {"tensor": tc})
+        w_one(2 * m + core)
 
     def w_mid():
-        for m in range(2):
-            got(dwr.at[m], dwsr.at[m], dwss.at[m], {"tensor": tc})
-        o = 1 - xlo
-        dws[...] = (dwp[2 * o + core].astype(f32) + dwr[o].astype(f32)).astype(bf16)
+        got(dwr.at[0], dwsr.at[0], dwss.at[0], {"tensor": tc})
+        dws[...] = (dwp[2 * far + core].astype(f32) + dwr[0].astype(f32)).astype(bf16)
         send(dws, dwx, dwss.at[2], dwsr.at[2], {"tensor": tx})
 
     def w_last():
+        got(dwr.at[1], dwsr.at[1], dwss.at[1], {"tensor": tc})
         got(dwx, dwsr.at[2], dwss.at[2], {"tensor": tx})
-        dw_o[...] = (dwp[2 * xlo + core].astype(f32) + dwr[xlo].astype(f32) + dwx[...].astype(f32)).astype(bf16)
+        dw_o[...] = (dwp[2 * xlo + core].astype(f32) + dwr[1].astype(f32) + dwx[...].astype(f32)).astype(bf16)
 
     ag_send(0)
-    tok_send((4, -4, 3, -3))
+    wave()
+    tok_send((6, 5, -5, 4, -4, 3, -3, 2, -2))
     l_f.wait()
     y_step(1)
     ag_step(1)
-    tok_send((2, -2, 1, -1))
     y_step(2)
     ag_step(2)
     got(wg.at[tx], wsr.at[0], wss.at[0], {"tensor": tx})
@@ -276,12 +285,13 @@
     k_step(4)
     dx_step(5)
     k_make(5)
+    w_pair(far, 0)
+    ya_step(2)
     k_step(5)
-    w_all()
-    ya_step(2)
-    dx_step(0)
     w_mid()
     ya_step(3)
+    w_pair(xlo, 1)
+    dx_step(0)
     k_last()
     l_o.wait()
     l_m.wait()
@@ -339,7 +349,7 @@
             DMA((6,)), DMA((11,)), DMA((11,)), DMA((3,)), DMA((3,)), DMA((3,)), DMA((3,)),
             DMA((2, 6)), DMA((2, 6)), DMA((11,)), DMA((11,)), DMA((2, 6)), DMA((2, 6)), DMA((3,)), DMA((3,)),
             DMA((3,)), DMA((3,)), DMA((2, 2, 4)), DMA((2, 2, 4)), DMA((2,)), DMA((2,)),
-            DMA((2, 2, 4)), DMA((2, 2, 4)),
+            DMA((2, 2, 4)), DMA((2, 2, 4)), pltpu.SemaphoreType.REGULAR((2, F // 2)),
         ],
         compiler_params=pltpu.CompilerParams(collective_id=0, has_side_effects=True,
                                              vmem_limit_bytes=40 << 20),

time: 74.4 us -> 80.7 us (1.085)
  the two profiles are of different devices: /device:TPU:29 before, /device:TPU:1 now
where the time goes in v3:
time: 80.7 us; the launch traced here: 80.6 us
  Pallas kernels  79.9 us (99%)
    pallas_call x1, Pallas kernels, body(): pl.pallas_call(kernel, out_shape=tuple((V(o.shape, o.dtype) for o in outs...  77.7 us
    pallas_call x1, Pallas kernels, body(): pl.pallas_call(flush, out_shape=outs, in_specs=[vmem] * 5, out_specs=(hbm...  2.25 us

profile of v3, /device:TPU:1, one launch (start us, length us, event | category | flops | bytes accessed | tf_op | source)
XLA Modules:
  0.0 80.6 jit_solution(17291501477651493551)
XLA Ops:
  0.6 77.7 %shard_map.101 = (bf16[128,256]{1,0:T(8,128)(2,1)S(1)}, bf16[32,6144]{1,0:T(8,128)(2,1)S(1)}, bf16[512,256]{1,0:T(8,128)(2,1)S(1)}, f32[8,2,64,512]{3,2,1,0:T(8,128)S(1)}, f32[8,2,64,512]{3,2,1,0:T(8,128)S(1)}) custom-call(bf16[128,6144]{1,0:T(8,128)(2,1)} %tok.1, bf16[512,256]{1,0:T(8,128)(2,1)} %bitcast.10, bf16[128,256]{1,0:T(8,128)(2,1)} %cot.1, ...), custom_call_target="tpu_custom_call" | custom-call | tf_op jit(solution)/shard_map/pallas_call | solution.py:336
  78.3 2.3 %shard_map.102 = (bf16[128,256]{1,0:T(8,128)(2,1)}, bf16[32,6144]{1,0:T(8,128)(2,1)}, bf16[512,256]{1,0:T(8,128)(2,1)}, f32[8,2,64,512]{3,2,1,0:T(8,128)}, f32[8,2,64,512]{3,2,1,0:T(8,128)}) custom-call(bf16[128,256]{1,0:T(8,128)(2,1)S(1)} %get-tuple-element.15.refs_0_, bf16[32,6144]{1,0:T(8,128)(2,1)S(1)} %get-tuple-element.16.refs_1_, ...), custom_call_target="tpu_custom_call" | custom-call | tf_op jit(solution)/shard_map/pallas_call | solution.py:357

commit v4 on v3

v4 whole, which is shorter than its diff:
```python
import jax
import jax.numpy as jnp
from jax import lax
from jax.experimental import pallas as pl
from jax.experimental.pallas import tpu as pltpu
from jax.sharding import PartitionSpec as P

outer_rate = 0.7
beta_outer = 0.9
MESH = pl.DeviceIdType.MESH
F, T, Y = 12, 4, 8
QR, DB, KT = 32, 512, 256
bf16, f32 = jnp.bfloat16, jnp.float32


def kernel(tok, w, cot, frag, outer, mom, keys_o, dx_o, dw_o, no_o, nm_o,
           xa, ca, wg, dxs, kp, kst, kl, kf, kfin, dwp, dwr, dws, dwx,
           fr, yss, yl, yf, ys, xr, sm, ov, mv,
           lsem, tks, tkr, cts, ctr, wss, wsr, ags, agr, dxsm, dxr, kss, ksr, kts, ktr,
           dwss, dwsr, yrs, yrrs, xss, xsr, yas, yar):
    isl = lax.axis_index("island")
    f = lax.axis_index("fsdp")
    t = lax.axis_index("tensor")
    y = lax.rem(isl, Y)
    xh = isl - y
    fz = lambda k: lax.rem(f + (k + F), F)
    ty = lambda k: lax.rem(t + (k + T), T)
    yy = lambda k: lax.rem(y + (k + 2 * Y), Y)
    yd = lambda k: {"island": xh + yy(k)}
    xpart = {"island": lax.rem(isl + Y, 2 * Y)}
    core = lax.rem(t, 2)
    xlo = lax.div(t, 2)
    tc = t + 1 - 2 * core
    tx = ty(2)
    pending = []

    def local(src, dst, sem):
        c = pltpu.make_async_copy(src, dst, sem)
        c.start()
        return c

    def rc(src, dst, ss, rs, dev):
        return pltpu.make_async_remote_copy(src_ref=src, dst_ref=dst, send_sem=ss, recv_sem=rs,
                                            device_id=dev, device_id_type=MESH)

    def send(*a):
        c = rc(*a)
        c.start()
        pending.append(c)

    def got(dst, rs, ss, dev):
        rc(dst, dst, ss, rs, dev).wait_recv()

    cot_rows = lambda q: cot.at[pl.ds(pl.multiple_of(q * QR, QR), QR), :]
    tok_blk = lambda b: tok.at[pl.ds(pl.multiple_of(t * QR, QR), QR), pl.ds(pl.multiple_of(b * DB, DB), DB)]
    dx_blk = lambda b: dx_o.at[:, pl.ds(pl.multiple_of(b * DB, DB), DB)]

    bar = pltpu.get_barrier_semaphore()
    peers = [{"fsdp": fz(k)} for k in range(1, F)] + [{"tensor": ty(k)} for k in range(1, T)]
    peers += [yd(1), yd(-1), yd(2), yd(-2), xpart]
    for d in peers:
        pl.semaphore_signal(bar, inc=1, device_id=d, device_id_type=MESH)

    l_w = local(w, wg.at[t], lsem.at[0])
    l_c = local(cot_rows(t), ca.at[f, t], lsem.at[1])
    l_x = local(tok_blk(f), xa.at[f], lsem.at[2])
    l_f = local(frag, fr, lsem.at[3])
    pl.semaphore_wait(bar, len(peers))

    for j in range(1, T):
        send(cot_rows(ty(j)), ca.at[f, t], cts.at[j - 1], ctr.at[j - 1], {"tensor": ty(j)})
    for h in range(2):
        four = 2 if h == 0 else -2
        send(frag.at[yy(4), h], yl.at[h, 2], yrs.at[h, 2], yrrs.at[h, 2], yd(four))
        send(frag.at[yy(3), h], yl.at[h, 0], yrs.at[h, 0], yrrs.at[h, 0], yd(1))
        send(frag.at[yy(-3), h], yl.at[h, 1], yrs.at[h, 1], yrrs.at[h, 1], yd(-1))
    for h in range(2):
        send(frag.at[yy(1), h], yf.at[h, 0], yrs.at[h, 3], yrrs.at[h, 3], yd(1))
        send(frag.at[yy(-1), h], yf.at[h, 1], yrs.at[h, 4], yrrs.at[h, 4], yd(-1))
    send(w, wg.at[t], wss.at[0], wsr.at[0], {"tensor": tx})
    send(w, wg.at[t], wss.at[1], wsr.at[1], {"tensor": tc})
    def tok_send(ks):
        for k in ks:
            b = fz(k)
            i = k % F - 1
            send(tok_blk(b), xa.at[f], tks.at[i], tkr.at[i], {"fsdp": b})

    tok_send((6, 5, -5))
    l_o = local(outer, ov, lsem.at[4])
    l_m = local(mom, mv, lsem.at[5])

    l_c.wait()
    for j in range(1, T):
        got(ca.at[f, ty(-j)], ctr.at[j - 1], cts.at[j - 1], {"tensor": ty(-j)})

    sg = 1 - 2 * core

    def ag_put(b, k, to):
        i = k % F - 1
        send(ca.at[b], ca.at[b], ags.at[i], agr.at[i], {"fsdp": fz(to)})

    def ag_got(*ks):
        for k in ks:
            i = k % F - 1
            got(ca.at[fz(-k)], agr.at[i], ags.at[i], {"fsdp": fz(-k)})

    def ag_first():
        for k in (3, -3, 2, -2, 1, -1):
            ag_put(f, k, k)

    def ag_pass():
        ag_got(3, -3)
        ag_put(fz(-3 * sg), 6, 3 * sg)
        for k in (5, -5, 4, -4):
            d = 3 if k > 0 else -3
            ag_put(fz(-d), k, k - d)

    def dx_step(s):
        ks = (-s, s) if s % 6 else (s,)
        bs = [fz(k) for k in ks]
        acc = None
        for q in range(T):
            lhs = jnp.concatenate([ca[b, q] for b in bs], axis=0) if len(bs) > 1 else ca[bs[0], q]
            p = lax.dot_general(lhs, wg[q], (((1,), (1,)), ((), ())), preferred_element_type=f32)
            acc = p if acc is None else acc + p
        for n, (k, b) in enumerate(zip(ks, bs)):
            r = acc[n * QR:(n + 1) * QR].astype(bf16)
            if k == 0:
                dx_o[:, pl.ds(pl.multiple_of(f * DB, DB), DB)] = r
            else:
                i = k % F - 1
                dxs[b] = r
                send(dxs.at[b], dx_blk(f), dxsm.at[i], dxr.at[i], {"fsdp": b})

    def y_got(ref, h, i):
        got(ref, yrrs.at[h, i], yrs.at[h, i], yd(1))
        return ref[...].astype(f32)

    def y_relay():
        for h in range(2):
            four = y_got(yl.at[h, 2], h, 2)
            for d, sgn in ((0, 1), (1, -1)):
                v = y_got(yl.at[h, d], h, d) + fr[yy(2 * sgn), h].astype(f32)
                if d == h:
                    v = v + four
                yss[h, d] = v.astype(bf16)
                send(yss.at[h, d], yf.at[h, 2 + d], yrs.at[h, 5 + d], yrrs.at[h, 5 + d], yd(2 * sgn))

    def y_last():
        for h in range(2):
            v = fr[y, h].astype(f32)
            for n in range(4):
                v = v + y_got(yf.at[h, n], h, 3 + n)
            ys[h] = v.astype(bf16)
            send(ys.at[h], xr.at[h], xss.at[h], xsr.at[h], xpart)

    def update(b, h):
        avg = ov[b, h] - sm[b, h].astype(f32) * (1.0 / (2 * Y))
        nm = beta_outer * mv[b, h] + avg
        nm_o[b, h] = nm
        no_o[b, h] = ov[b, h] - outer_rate * (avg + beta_outer * nm)

    def ya_put(b, h, k, to):
        i = k % Y - 1
        send(sm.at[b, h], sm.at[b, h], yas.at[h, i], yar.at[h, i], yd(to))

    def ya_got(h, k):
        i = k % Y - 1
        got(sm.at[yy(-k), h], yar.at[h, i], yas.at[h, i], yd(1))

    def ya_first():
        for h in range(2):
            got(xr.at[h], xsr.at[h], xss.at[h], xpart)
            sm[y, h] = (ys[h].astype(f32) + xr[h].astype(f32)).astype(bf16)
            for k in (2, -2, 1, -1):
                ya_put(y, h, k, k)

    def ya_pass():
        for h in range(2):
            ya_got(h, 2)
            ya_got(h, -2)
            ya_put(yy(-2 if h == 0 else 2), h, 4, 2 if h == 0 else -2)
            ya_put(yy(-2), h, 3, 1)
            ya_put(yy(2), h, -3, -1)

    def upd(*ks):
        for h in range(2):
            for k in ks:
                if k not in (0, 2, -2):
                    ya_got(h, k)
                update(yy(-k), h)

    def k_make(*ks):
        for k in ks:
            if k == 0:
                l_x.wait()
            else:
                i = (-k) % F - 1
                got(xa.at[fz(k)], tkr.at[i], tks.at[i], {"fsdp": fz(k)})
        bs = [fz(k) for k in ks]
        lhs = jnp.concatenate([xa[b] for b in bs], axis=0) if len(bs) > 1 else xa[bs[0]]
        for q in range(T):
            r = jnp.dot(lhs, wg[q], preferred_element_type=f32)
            for n, k in enumerate(ks):
                v = r[n * QR:(n + 1) * QR]
                if k in (0, 3, -3):
                    kp[q, (0, 3, -3).index(k)] = v
                else:
                    kst[k % F, q] = v.astype(bf16)

    def k_leaf():
        k_make(6)
        send(kst.at[6], kl.at[2, 0], kss.at[6], ksr.at[6], {"fsdp": fz(3 * sg)})
        for j in (2, 1):
            k_make(3 + j, -3 - j)
            for d, sgn in ((0, 1), (1, -1)):
                k = sgn * (3 + j)
                send(kst.at[k % F], kl.at[d, j - 1], kss.at[k % F], ksr.at[k % F], {"fsdp": fz(sgn * j)})

    def k_near(j):
        k_make(j, -j)
        for d, sgn in ((0, 1), (1, -1)):
            k = sgn * j
            send(kst.at[k % F], kf.at[d, j - 1], kss.at[k % F], ksr.at[k % F], {"fsdp": fz(k)})

    def k_relay():
        got(kl.at[2, 0], ksr.at[6], kss.at[6], {"fsdp": fz(-3)})
        for d, sgn in ((0, 1), (1, -1)):
            v = kp[:, 1 + d]
            for j in (1, 2):
                k = (sgn * (3 + j)) % F
                got(kl.at[d, j - 1], ksr.at[k], kss.at[k], {"fsdp": fz(-sgn * j)})
                v = v + kl[d, j - 1].astype(f32)
            here = (core == d).astype(f32)
            v = v + here * kl[2, 0].astype(f32)
            k = (3 * sgn) % F
            kst[k] = v.astype(bf16)
            send(kst.at[k], kf.at[d, 2], kss.at[k], ksr.at[k], {"fsdp": fz(3 * sgn)})

    def k_last():
        v = kp[:, 0]
        for j in (1, 2, 3):
            for d, sgn in ((0, 1), (1, -1)):
                k = (sgn * j) % F
                got(kf.at[d, j - 1], ksr.at[k], kss.at[k], {"fsdp": fz(-sgn * j)})
                v = v + kf[d, j - 1].astype(f32)
        kfin[...] = v.astype(bf16)
        rows = pl.ds(pl.multiple_of(t * QR, QR), QR)
        mine = keys_o.at[rows, :]
        for j in range(1, T):
            q = ty(j)
            send(kfin.at[q], mine, kts.at[j - 1], ktr.at[j - 1], {"tensor": q})
        keys_o[rows, :] = kfin[t]

    far = 1 - xlo

    def w_one(q):
        r = lax.dot_general(xa[...].reshape(F * QR, DB), ca[:, q].reshape(F * QR, KT),
                            (((0,), (0,)), ((), ())), preferred_element_type=f32)
        dwp[q] = r.astype(bf16)

    def w_pair(m, i):
        w_one(2 * m + 1 - core)
        send(dwp.at[2 * m + 1 - core], dwr.at[i], dwss.at[i], dwsr.at[i], {"tensor": tc})
        w_one(2 * m + core)

    def w_mid():
        got(dwr.at[0], dwsr.at[0], dwss.at[0], {"tensor": tc})
        dws[...] = (dwp[2 * far + core].astype(f32) + dwr[0].astype(f32)).astype(bf16)
        send(dws, dwx, dwss.at[2], dwsr.at[2], {"tensor": tx})

    def w_last():
        got(dwr.at[1], dwsr.at[1], dwss.at[1], {"tensor": tc})
        got(dwx, dwsr.at[2], dwss.at[2], {"tensor": tx})
        dw_o[...] = (dwp[2 * xlo + core].astype(f32) + dwr[1].astype(f32) + dwx[...].astype(f32)).astype(bf16)

    ag_first()
    tok_send((4, -4, 3, -3))
    l_f.wait()
    y_relay()
    ag_pass()
    tok_send((2, -2, 1, -1))
    got(wg.at[tx], wsr.at[0], wss.at[0], {"tensor": tx})
    send(wg.at[tx], wg.at[tx], wss.at[2], wsr.at[2], {"tensor": tc})
    l_w.wait()
    got(wg.at[tc], wsr.at[1], wss.at[1], {"tensor": tc})
    txc = lax.rem(tc + 2, T)
    got(wg.at[txc], wsr.at[2], wss.at[2], {"tensor": tc})
    k_leaf()
    y_last()
    dx_step(3)
    k_make(3, -3)
    ag_got(2, -2, 1, -1)
    k_relay()
    dx_step(2)
    k_near(2)
    ya_first()
    k_near(1)
    dx_step(1)
    ag_got(6, 5, -5, 4, -4)
    dx_step(6)
    dx_step(5)
    dx_step(4)
    k_make(0)
    w_pair(far, 0)
    ya_pass()
    k_last()
    w_mid()
    w_pair(xlo, 1)
    dx_step(0)
    l_o.wait()
    l_m.wait()
    upd(0, 2, -2)
    upd(1, -1)
    upd(3, -3)
    upd(4)
    w_last()
    for k in range(1, F):
        got(dx_blk(fz(-k)), dxr.at[k - 1], dxsm.at[k - 1], {"fsdp": fz(-k)})
    for j in range(1, T):
        q = ty(-j)
        got(keys_o.at[pl.ds(pl.multiple_of(q * QR, QR), QR), :], ktr.at[j - 1], kts.at[j - 1], {"tensor": q})
    for c in pending:
        c.wait_send()


def flush(*refs):
    n = len(refs) // 2
    sem = refs[-1]
    copies = [pltpu.make_async_copy(refs[i], refs[n + i], sem.at[i]) for i in (3, 4, 1, 2, 0)]
    for c in copies:
        c.start()
    for c in copies:
        c.wait()


def body(tokens, key_weight, key_cotangent, local_frag, outer_frag, momentum):
    FS = (Y, 2, 64, 512)
    V, DMA = pltpu.VMEM, pltpu.SemaphoreType.DMA
    blk = (T, QR, KT)
    hbm = pl.BlockSpec(memory_space=pltpu.HBM)
    vmem = pl.BlockSpec(memory_space=pltpu.VMEM)
    outs = (
        jax.ShapeDtypeStruct((T * QR, KT), bf16),
        jax.ShapeDtypeStruct((QR, F * DB), bf16),
        jax.ShapeDtypeStruct((DB, KT), bf16),
        jax.ShapeDtypeStruct(FS, f32),
        jax.ShapeDtypeStruct(FS, f32),
    )
    fixed = lambda a: pltpu.with_memory_space_constraint(a, pltpu.HBM)
    made = pl.pallas_call(
        kernel,
        out_shape=tuple(V(o.shape, o.dtype) for o in outs),
        in_specs=[hbm] * 6,
        out_specs=(vmem,) * 5,
        scratch_shapes=[
            V((F, QR, DB), bf16), V((F,) + blk, bf16), V((T, DB, KT), bf16), V((F, QR, DB), bf16),
            V((T, 3, QR, KT), f32), V((F,) + blk, bf16), V((3, 2) + blk, bf16), V((2, 3) + blk, bf16), V(blk, bf16),
            V((T, DB, KT), bf16), V((2, DB, KT), bf16), V((DB, KT), bf16), V((DB, KT), bf16),
            V(FS, bf16), V((2, 2, 64, 512), bf16), V((2, 3, 64, 512), bf16), V((2, 4, 64, 512), bf16),
            V((2, 64, 512), bf16), V((2, 64, 512), bf16), V(FS, bf16),
            V(FS, f32), V(FS, f32),
            DMA((6,)), DMA((11,)), DMA((11,)), DMA((3,)), DMA((3,)), DMA((3,)), DMA((3,)),
            DMA((11,)), DMA((11,)), DMA((11,)), DMA((11,)), DMA((F,)), DMA((F,)), DMA((3,)), DMA((3,)),
            DMA((3,)), DMA((3,)), DMA((2, 7)), DMA((2, 7)), DMA((2,)), DMA((2,)),
            DMA((2, 7)), DMA((2, 7)),
        ],
        compiler_params=pltpu.CompilerParams(collective_id=0, has_side_effects=True,
                                             vmem_limit_bytes=40 << 20),
    )(*map(fixed, (tokens, key_weight[0], key_cotangent, local_frag.reshape(FS), outer_frag.reshape(FS), momentum.reshape(FS))))
    keys, dx, dw, no, nm = pl.pallas_call(
        flush,
        out_shape=outs,
        in_specs=[vmem] * 5,
        out_specs=(hbm,) * 5,
        scratch_shapes=[DMA((5,))],
        compiler_params=pltpu.CompilerParams(vmem_limit_bytes=1 << 20),
    )(*made)
    return keys, dx, dw[None], no.reshape(outer_frag.shape), nm.reshape(momentum.shape)


def solution(mesh):
    return jax.shard_map(
        body,
        mesh=mesh,
        in_specs=(
            P(("island", "fsdp"), None),
            P("island", "fsdp", "tensor"),
            P(("island", "fsdp"), "tensor"),
            P("island", None, "fsdp", "tensor"),
            P(None, "fsdp", "tensor"),
            P(None, "fsdp", "tensor"),
        ),
        out_specs=(
            P(("island", "fsdp"), "tensor"),
            P(("island", "fsdp", "tensor"), None),
            P("island", "fsdp", "tensor"),
            P(None, "fsdp", "tensor"),
            P(None, "fsdp", "tensor"),
        ),
        check_vma=False,
    )
```

time: 80.7 us -> 80 us (level)
  the two profiles are of different devices: /device:TPU:1 before, /device:TPU:21 now
where the time goes in v4:
time: 80 us; the launch traced here: 79.9 us
  Pallas kernels  79.3 us (99%)
    pallas_call x1, Pallas kernels, body(): pl.pallas_call(kernel, out_shape=tuple((V(o.shape, o.dtype) for o in outs...  77 us
    pallas_call x1, Pallas kernels, body(): pl.pallas_call(flush, out_shape=outs, in_specs=[vmem] * 5, out_specs=(hbm...  2.25 us

profile of v4, /device:TPU:21, one launch (start us, length us, event | category | flops | bytes accessed | tf_op | source)
XLA Modules:
  0.0 79.9 jit_solution(12791179592114857256)
XLA Ops:
  0.6 77.0 %shard_map.101 = (bf16[128,256]{1,0:T(8,128)(2,1)S(1)}, bf16[32,6144]{1,0:T(8,128)(2,1)S(1)}, bf16[512,256]{1,0:T(8,128)(2,1)S(1)}, f32[8,2,64,512]{3,2,1,0:T(8,128)S(1)}, f32[8,2,64,512]{3,2,1,0:T(8,128)S(1)}) custom-call(bf16[128,6144]{1,0:T(8,128)(2,1)} %tok.1, bf16[512,256]{1,0:T(8,128)(2,1)} %bitcast.10, bf16[128,256]{1,0:T(8,128)(2,1)} %cot.1, ...), custom_call_target="tpu_custom_call" | custom-call | tf_op jit(solution)/shard_map/pallas_call | solution.py:351
  77.6 2.3 %shard_map.102 = (bf16[128,256]{1,0:T(8,128)(2,1)}, bf16[32,6144]{1,0:T(8,128)(2,1)}, bf16[512,256]{1,0:T(8,128)(2,1)}, f32[8,2,64,512]{3,2,1,0:T(8,128)}, f32[8,2,64,512]{3,2,1,0:T(8,128)}) custom-call(bf16[128,256]{1,0:T(8,128)(2,1)S(1)} %get-tuple-element.15.refs_0_, bf16[32,6144]{1,0:T(8,128)(2,1)S(1)} %get-tuple-element.16.refs_1_, ...), custom_call_target="tpu_custom_call" | custom-call | tf_op jit(solution)/shard_map/pallas_call | solution.py:371

commit v5 on v3

--- a/solution.py
+++ b/solution.py
@@ -21,7 +21,7 @@
            xa, ca, wg, dxs, kp, ksp, ksm, krp, krm, kfin, dwp, dwr, dws, dwx,
            fr, yss, yrr, ys, xr, sm, ov, mv,
            lsem, tks, tkr, cts, ctr, wss, wsr, ags, agr, dxsm, dxr, kss, ksr, kts, ktr,
-           dwss, dwsr, yrs, yrrs, xss, xsr, yas, yar, wv):
+           dwss, dwsr, yrs, yrrs, xss, xsr, yas, yar):
     isl = lax.axis_index("island")
     f = lax.axis_index("fsdp")
     t = lax.axis_index("tensor")
@@ -60,7 +60,7 @@
     dx_blk = lambda b: dx_o.at[:, pl.ds(pl.multiple_of(b * DB, DB), DB)]
 
     bar = pltpu.get_barrier_semaphore()
-    peers = [{"fsdp": fz(1)}, {"fsdp": fz(-1)}] + [{"tensor": ty(k)} for k in range(1, T)]
+    peers = [{"fsdp": fz(k)} for k in range(1, F)] + [{"tensor": ty(k)} for k in range(1, T)]
     peers += [yd(1), yd(-1), xpart]
     for d in peers:
         pl.semaphore_signal(bar, inc=1, device_id=d, device_id_type=MESH)
@@ -84,15 +84,7 @@
             i = k % F - 1
             send(tok_blk(b), xa.at[f], tks.at[i], tkr.at[i], {"fsdp": b})
 
-    def wave():
-        for n in range(F // 2):
-            for d, sgn in ((0, 1), (1, -1)):
-                if n > 0:
-                    pl.semaphore_wait(wv.at[d, n - 1], 1)
-                if n < F // 2 - 1:
-                    pl.semaphore_signal(wv.at[d, n], inc=1, device_id={"fsdp": fz(sgn)}, device_id_type=MESH)
-
-    tok_send((1, -1))
+    tok_send((6, 5, -5))
     l_o = local(outer, ov, lsem.at[4])
     l_m = local(mom, mv, lsem.at[5])
 
@@ -247,11 +239,11 @@
         dw_o[...] = (dwp[2 * xlo + core].astype(f32) + dwr[1].astype(f32) + dwx[...].astype(f32)).astype(bf16)
 
     ag_send(0)
-    wave()
-    tok_send((6, 5, -5, 4, -4, 3, -3, 2, -2))
+    tok_send((4, -4, 3, -3))
     l_f.wait()
     y_step(1)
     ag_step(1)
+    tok_send((2, -2, 1, -1))
     y_step(2)
     ag_step(2)
     got(wg.at[tx], wsr.at[0], wss.at[0], {"tensor": tx})
@@ -349,7 +341,7 @@
             DMA((6,)), DMA((11,)), DMA((11,)), DMA((3,)), DMA((3,)), DMA((3,)), DMA((3,)),
             DMA((2, 6)), DMA((2, 6)), DMA((11,)), DMA((11,)), DMA((2, 6)), DMA((2, 6)), DMA((3,)), DMA((3,)),
             DMA((3,)), DMA((3,)), DMA((2, 2, 4)), DMA((2, 2, 4)), DMA((2,)), DMA((2,)),
-            DMA((2, 2, 4)), DMA((2, 2, 4)), pltpu.SemaphoreType.REGULAR((2, F // 2)),
+            DMA((2, 2, 4)), DMA((2, 2, 4)),
         ],
         compiler_params=pltpu.CompilerParams(collective_id=0, has_side_effects=True,
                                              vmem_limit_bytes=40 << 20),

time: 80.7 us -> 70.2 us (0.87)
  Pallas kernels: 79.9 us -> 69.5 us
    pallas_call x1, Pallas kernels: 77.7 us -> 67.2 us  [body(): pl.pallas_call(kernel, out_shape=tuple((V(o.shape, o.dtype) for o in outs...]
where the time goes in v5:
time: 70.2 us; the launch traced here: 70.1 us
  Pallas kernels  69.5 us (99%)
    pallas_call x1, Pallas kernels, body(): pl.pallas_call(kernel, out_shape=tuple((V(o.shape, o.dtype) for o in outs...  67.2 us
    pallas_call x1, Pallas kernels, body(): pl.pallas_call(flush, out_shape=outs, in_specs=[vmem] * 5, out_specs=(hbm...  2.25 us

profile of v5, /device:TPU:1, one launch (start us, length us, event | category | flops | bytes accessed | tf_op | source)
XLA Modules:
  0.0 70.1 jit_solution(4342883802321966307)
XLA Ops:
  0.6 67.2 %shard_map.101 = (bf16[128,256]{1,0:T(8,128)(2,1)S(1)}, bf16[32,6144]{1,0:T(8,128)(2,1)S(1)}, bf16[512,256]{1,0:T(8,128)(2,1)S(1)}, f32[8,2,64,512]{3,2,1,0:T(8,128)S(1)}, f32[8,2,64,512]{3,2,1,0:T(8,128)S(1)}) custom-call(bf16[128,6144]{1,0:T(8,128)(2,1)} %tok.1, bf16[512,256]{1,0:T(8,128)(2,1)} %bitcast.10, bf16[128,256]{1,0:T(8,128)(2,1)} %cot.1, ...), custom_call_target="tpu_custom_call" | custom-call | tf_op jit(solution)/shard_map/pallas_call | solution.py:328
  67.9 2.3 %shard_map.102 = (bf16[128,256]{1,0:T(8,128)(2,1)}, bf16[32,6144]{1,0:T(8,128)(2,1)}, bf16[512,256]{1,0:T(8,128)(2,1)}, f32[8,2,64,512]{3,2,1,0:T(8,128)}, f32[8,2,64,512]{3,2,1,0:T(8,128)}) custom-call(bf16[128,256]{1,0:T(8,128)(2,1)S(1)} %get-tuple-element.15.refs_0_, bf16[32,6144]{1,0:T(8,128)(2,1)S(1)} %get-tuple-element.16.refs_1_, ...), custom_call_target="tpu_custom_call" | custom-call | tf_op jit(solution)/shard_map/pallas_call | solution.py:349

commit v6 on v5

--- a/solution.py
+++ b/solution.py
@@ -255,26 +255,26 @@
     k_make(0)
     k_step(0)
     dx_step(1)
+    k_make(1)
     y_step(3)
     ag_step(3)
-    k_make(1)
     k_step(1)
     dx_step(2)
+    k_make(2)
     y_last()
     ag_step(4)
-    k_make(2)
     k_step(2)
     dx_step(3)
+    k_make(3)
     ya_first()
     ag_step(5)
-    k_make(3)
     k_step(3)
     dx_step(4)
+    k_make(4)
     ya_step(1)
     ag_step(6)
+    k_step(4)
     dx_step(6)
-    k_make(4)
-    k_step(4)
     dx_step(5)
     k_make(5)
     w_pair(far, 0)

time: 70.2 us -> 70.9 us (level)
  no operation moved by 1% of the time
where the time goes in v6:
time: 70.9 us; the launch traced here: 70.1 us
  Pallas kernels  69.5 us (98%)
    pallas_call x1, Pallas kernels, body(): pl.pallas_call(kernel, out_shape=tuple((V(o.shape, o.dtype) for o in outs...  67.2 us
    pallas_call x1, Pallas kernels, body(): pl.pallas_call(flush, out_shape=outs, in_specs=[vmem] * 5, out_specs=(hbm...  2.25 us

profile of v6, /device:TPU:1, one launch (start us, length us, event | category | flops | bytes accessed | tf_op | source)
XLA Modules:
  0.0 70.1 jit_solution(8376006150517905568)
XLA Ops:
  0.6 67.2 %shard_map.101 = (bf16[128,256]{1,0:T(8,128)(2,1)S(1)}, bf16[32,6144]{1,0:T(8,128)(2,1)S(1)}, bf16[512,256]{1,0:T(8,128)(2,1)S(1)}, f32[8,2,64,512]{3,2,1,0:T(8,128)S(1)}, f32[8,2,64,512]{3,2,1,0:T(8,128)S(1)}) custom-call(bf16[128,6144]{1,0:T(8,128)(2,1)} %tok.1, bf16[512,256]{1,0:T(8,128)(2,1)} %bitcast.10, bf16[128,256]{1,0:T(8,128)(2,1)} %cot.1, ...), custom_call_target="tpu_custom_call" | custom-call | tf_op jit(solution)/shard_map/pallas_call | solution.py:328
  67.9 2.3 %shard_map.102 = (bf16[128,256]{1,0:T(8,128)(2,1)}, bf16[32,6144]{1,0:T(8,128)(2,1)}, bf16[512,256]{1,0:T(8,128)(2,1)}, f32[8,2,64,512]{3,2,1,0:T(8,128)}, f32[8,2,64,512]{3,2,1,0:T(8,128)}) custom-call(bf16[128,256]{1,0:T(8,128)(2,1)S(1)} %get-tuple-element.15.refs_0_, bf16[32,6144]{1,0:T(8,128)(2,1)S(1)} %get-tuple-element.16.refs_1_, ...), custom_call_target="tpu_custom_call" | custom-call | tf_op jit(solution)/shard_map/pallas_call | solution.py:349
